TPU v7x, 32 devices: a whole 2x2x4 slice. The times are simulated.
32 devices in a mesh: dp: 8 (over z, y), mp: 4 (over x, core).
Axes of the slice: x: 2, y: 2, z: 4, core: 2. Of those that a mesh axis runs over, the one named last changes fastest.
Arguments:
- tokens: bfloat16 [4096, 2048], P('dp'), may hold values from -6 to 6
- text: bfloat16 [2048, 4096], P('dp', 'mp'), may hold values from -6 to 6
- image_seg: int32 [8, 512], P('dp'), may hold values from 0 to 1, never falling along the last dimension, each value on 1 to 320 neighbouring positions
- text_seg: int32 [8, 256], P('dp'), may hold values from 0 to 1, never falling along the last dimension, each value on 1 to 160 neighbouring positions
- w_qkv: bfloat16 [3, 2048, 2048], P(None, 'dp', 'mp'), may hold values from -0.125 to 0.125
- w_out: bfloat16 [2048, 2048], P('mp', 'dp'), may hold values from -1 to 1
- c_q: bfloat16 [2048, 2048], P('dp', 'mp'), may hold values from -0.125 to 0.125
- c_kv: bfloat16 [2, 4096, 2048], P(None, 'dp', 'mp'), may hold values from -0.09375 to 0.09375
- c_out: bfloat16 [2048, 2048], P('mp', 'dp'), may hold values from -1 to 1
- w_up: bfloat16 [2048, 8192], P('dp', 'mp'), may hold values from -0.125 to 0.125
- w_down: bfloat16 [8192, 2048], P('mp', 'dp'), may hold values from -0.0625 to 0.0625
- norm_gain: float32 [4, 2048], replicated, may hold values from 0.25 to 1.75
- norm_bias: float32 [4, 2048], replicated, may hold values from -4 to 4
- out_bias: float32 [3, 2048], replicated, may hold values from -4 to 4
- up_bias: float32 [8192], P('mp'), may hold values from -4 to 4
- cotangent: bfloat16 [4096, 2048], P('dp'), may hold values from -6 to 6
Outputs:
- output: bfloat16 [4096, 2048], P('dp')
- grad_tokens: float32 [4096, 2048], P('dp')
- grad_text: float32 [2048, 4096], P('dp', 'mp')
- grad_w_qkv: float32 [3, 2048, 2048], P(None, 'dp', 'mp')
- grad_w_out: float32 [2048, 2048], P('mp', 'dp')
- grad_c_q: float32 [2048, 2048], P('dp', 'mp')
- grad_c_kv: float32 [2, 4096, 2048], P(None, 'dp', 'mp')
- grad_c_out: float32 [2048, 2048], P('mp', 'dp')
- grad_w_up: float32 [2048, 8192], P('dp', 'mp')
- grad_w_down: float32 [8192, 2048], P('mp', 'dp')
- grad_norm_gain: float32 [4, 2048], replicated
- grad_norm_bias: float32 [4, 2048], replicated
- grad_out_bias: float32 [3, 2048], replicated
- grad_up_bias: float32 [8192], P('mp')
Inputs may be any that keep to these rules, and one draw needn't show every extreme that they name: In each row image_seg is 0 on the first image and 1 on the second; both images are present, and none has more than 320 tokens. In each row text_seg is 0 on the first caption and 1 on the second; both captions are present, and none has more than 160 tokens.
All inputs are finite; a program needn't handle non-finite values.
Results may differ from a plain program's by a relative error of at most 0.02.
Values may be sent and summed in bfloat16 or wider, within the bound.
No kernel may reach another device: no remote copies, remote signals or barrier semaphores. Data moves between devices by JAX's collectives and lax.ppermute only.
A program may use at most 256 MiB of HBM per device.

v0:
```python
import jax
import jax.numpy as jnp
from jax import lax
from jax.sharding import PartitionSpec as P

HD = 128
eps = 1e-05
masked = -1e30


def normalize(values, gain, shift):
    center = values - jnp.mean(values, axis=-1, keepdims=True)
    spread = jnp.mean(center * center, axis=-1, keepdims=True)
    return center * lax.rsqrt(spread + eps) * gain + shift


def gelu_tanh(values):
    return (
        0.5
        * values
        * (1.0 + jnp.tanh(0.7978845608028654 * (values + 0.044715 * values * values * values)))
    )


def heads_sum(partial_value):
    return lax.psum(partial_value, "mp")


def input_sum(partial_value):
    return lax.psum(partial_value, "mp")


def split_heads(values):
    return values.reshape(values.shape[0], values.shape[1] // HD, HD)


def scores_of(queries, key_rows, allowed):
    raw = jnp.einsum(
        "qhd,khd->hqk",
        split_heads(queries),
        split_heads(key_rows),
        preferred_element_type=jnp.float32,
    ) * HD ** (-0.5)
    return jnp.where(allowed[None], raw, masked)


def attend_forward(queries, key_rows, value_rows, allowed):
    scores = scores_of(queries, key_rows, allowed)
    top = jnp.max(scores, axis=-1, keepdims=True)
    expo = jnp.exp(scores - top)
    total = jnp.sum(expo, axis=-1, keepdims=True)
    probs = (expo / total).astype(jnp.bfloat16)
    mixed = jnp.einsum(
        "hqk,khd->qhd", probs, split_heads(value_rows), preferred_element_type=jnp.float32
    )
    return (
        mixed.reshape(queries.shape[0], queries.shape[1]).astype(jnp.bfloat16),
        top + jnp.log(total),
    )


def attend_backward(queries, key_rows, value_rows, grad_mixed, logsum, allowed):
    scores = scores_of(queries, key_rows, allowed)
    probs = jnp.exp(scores - logsum)
    grad_heads = split_heads(grad_mixed)
    grad_values = jnp.einsum(
        "hqk,qhd->khd", probs.astype(jnp.bfloat16), grad_heads, preferred_element_type=jnp.float32
    )
    grad_probs = jnp.einsum(
        "qhd,khd->hqk", grad_heads, split_heads(value_rows), preferred_element_type=jnp.float32
    )
    grad_scores = (
        probs * (grad_probs - jnp.sum(probs * grad_probs, axis=-1, keepdims=True))
    ).astype(jnp.bfloat16)
    grad_queries = jnp.einsum(
        "hqk,khd->qhd", grad_scores, split_heads(key_rows), preferred_element_type=jnp.float32
    ) * HD ** (-0.5)
    grad_keys = jnp.einsum(
        "hqk,qhd->khd", grad_scores, split_heads(queries), preferred_element_type=jnp.float32
    ) * HD ** (-0.5)
    return (
        grad_queries.reshape(queries.shape),
        grad_keys.reshape(key_rows.shape),
        grad_values.reshape(value_rows.shape),
    )


def on_device(
    tokens,
    text,
    image_seg,
    text_seg,
    w_qkv,
    w_out,
    c_q,
    c_kv,
    c_out,
    w_up,
    w_down,
    norm_gain,
    norm_bias,
    out_bias,
    up_bias,
    cotangent,
):
    row_count = image_seg.shape[0]
    length = image_seg.shape[1]
    text_len = text_seg.shape[1]
    gathered = (
        lax.all_gather(w_qkv, "dp", axis=1, tiled=True),
        lax.all_gather(w_out, "dp", axis=1, tiled=True),
        lax.all_gather(c_q, "dp", axis=0, tiled=True),
        lax.all_gather(c_kv, "dp", axis=1, tiled=True),
        lax.all_gather(c_out, "dp", axis=1, tiled=True),
        lax.all_gather(w_up, "dp", axis=0, tiled=True),
        lax.all_gather(w_down, "dp", axis=1, tiled=True),
    )
    full_qkv, full_out, full_cq, full_ckv, full_cout, full_up, full_down = gathered
    words = lax.all_gather(text, "mp", axis=1, tiled=True)
    same_image = image_seg[:, :, None] == image_seg[:, None, :]
    caption = image_seg[:, :, None] == text_seg[:, None, :]
    residual = tokens.astype(jnp.float32)
    width = full_qkv.shape[2]
    normed_one, pull_one = jax.vjp(normalize, residual, norm_gain[0], norm_bias[0])
    hidden_one = normed_one.astype(jnp.bfloat16)
    projected = jnp.einsum(
        "td,cde->cte", hidden_one, full_qkv, preferred_element_type=jnp.float32
    ).astype(jnp.bfloat16)
    self_inputs = (
        projected[0].reshape(row_count, length, width),
        projected[1].reshape(row_count, length, width),
        projected[2].reshape(row_count, length, width),
    )
    self_mixed, self_logsum = lax.map(
        lambda pieces: attend_forward(*pieces), self_inputs + (same_image,)
    )
    self_flat = self_mixed.reshape(row_count * length, width)
    after_self = (
        residual
        + heads_sum(jnp.dot(self_flat, full_out, preferred_element_type=jnp.float32))
        + out_bias[0]
    )
    normed_two, pull_two = jax.vjp(normalize, after_self, norm_gain[1], norm_bias[1])
    hidden_two = normed_two.astype(jnp.bfloat16)
    cross_query = jnp.dot(hidden_two, full_cq, preferred_element_type=jnp.float32).astype(
        jnp.bfloat16
    )
    text_kv = jnp.einsum("td,cde->cte", words, full_ckv, preferred_element_type=jnp.float32).astype(
        jnp.bfloat16
    )
    cross_inputs = (
        cross_query.reshape(row_count, length, width),
        text_kv[0].reshape(row_count, text_len, width),
        text_kv[1].reshape(row_count, text_len, width),
    )
    cross_mixed, cross_logsum = lax.map(
        lambda pieces: attend_forward(*pieces), cross_inputs + (caption,)
    )
    cross_flat = cross_mixed.reshape(row_count * length, width)
    after_cross = (
        after_self
        + heads_sum(jnp.dot(cross_flat, full_cout, preferred_element_type=jnp.float32))
        + out_bias[1]
    )
    normed_three, pull_three = jax.vjp(normalize, after_cross, norm_gain[2], norm_bias[2])
    hidden_three = normed_three.astype(jnp.bfloat16)
    pre_act = jnp.dot(hidden_three, full_up, preferred_element_type=jnp.float32) + up_bias
    activated, pull_gelu = jax.vjp(gelu_tanh, pre_act)
    act_low = activated.astype(jnp.bfloat16)
    after_mlp = (
        after_cross
        + heads_sum(jnp.dot(act_low, full_down, preferred_element_type=jnp.float32))
        + out_bias[2]
    )
    final, pull_four = jax.vjp(normalize, after_mlp, norm_gain[3], norm_bias[3])
    output = final.astype(jnp.bfloat16)
    grad_mlp, gain_four, shift_four = pull_four(cotangent.astype(jnp.float32))
    grad_mlp_low = grad_mlp.astype(jnp.bfloat16)
    grad_down = jnp.einsum("tf,td->fd", act_low, grad_mlp_low, preferred_element_type=jnp.float32)
    grad_act = jnp.einsum("td,fd->tf", grad_mlp_low, full_down, preferred_element_type=jnp.float32)
    grad_pre = pull_gelu(grad_act)[0].astype(jnp.bfloat16)
    up_bias_grad = jnp.sum(grad_pre.astype(jnp.float32), axis=0)
    grad_up = jnp.einsum("td,tf->df", hidden_three, grad_pre, preferred_element_type=jnp.float32)
    grad_hidden_three = input_sum(
        jnp.einsum("tf,df->td", grad_pre, full_up, preferred_element_type=jnp.float32)
    )
    grad_cross_in, gain_three, shift_three = pull_three(grad_hidden_three)
    grad_after_cross = grad_mlp + grad_cross_in
    grad_cross_low = grad_after_cross.astype(jnp.bfloat16)
    grad_cout = jnp.einsum(
        "te,td->ed", cross_flat, grad_cross_low, preferred_element_type=jnp.float32
    )
    grad_cmix = jnp.einsum(
        "td,ed->te", grad_cross_low, full_cout, preferred_element_type=jnp.float32
    ).astype(jnp.bfloat16)
    cq_grad, ck_grad, cv_grad = lax.map(
        lambda pieces: attend_backward(*pieces),
        cross_inputs + (grad_cmix.reshape(row_count, length, width), cross_logsum, caption),
    )
    cq_low = cq_grad.reshape(row_count * length, width).astype(jnp.bfloat16)
    ckv_low = jnp.stack(
        [ck_grad.reshape(row_count * text_len, width), cv_grad.reshape(row_count * text_len, width)]
    ).astype(jnp.bfloat16)
    grad_cq = jnp.einsum("td,te->de", hidden_two, cq_low, preferred_element_type=jnp.float32)
    grad_ckv = jnp.einsum("td,cte->cde", words, ckv_low, preferred_element_type=jnp.float32)
    text_term = jnp.einsum("cte,cde->td", ckv_low, full_ckv, preferred_element_type=jnp.float32)
    grad_text = lax.psum_scatter(
        text_term.astype(jnp.bfloat16), "mp", scatter_dimension=1, tiled=True
    ).astype(jnp.float32)
    grad_hidden_two = input_sum(
        jnp.einsum("te,de->td", cq_low, full_cq, preferred_element_type=jnp.float32)
    )
    grad_self_in, gain_two, shift_two = pull_two(grad_hidden_two)
    grad_after_self = grad_after_cross + grad_self_in
    grad_self_low = grad_after_self.astype(jnp.bfloat16)
    grad_wout = jnp.einsum(
        "te,td->ed", self_flat, grad_self_low, preferred_element_type=jnp.float32
    )
    grad_smix = jnp.einsum(
        "td,ed->te", grad_self_low, full_out, preferred_element_type=jnp.float32
    ).astype(jnp.bfloat16)
    sq_grad, sk_grad, sv_grad = lax.map(
        lambda pieces: attend_backward(*pieces),
        self_inputs + (grad_smix.reshape(row_count, length, width), self_logsum, same_image),
    )
    qkv_low = jnp.stack(
        [
            sq_grad.reshape(row_count * length, width),
            sk_grad.reshape(row_count * length, width),
            sv_grad.reshape(row_count * length, width),
        ]
    ).astype(jnp.bfloat16)
    grad_qkv = jnp.einsum("td,cte->cde", hidden_one, qkv_low, preferred_element_type=jnp.float32)
    grad_hidden_one = input_sum(
        jnp.einsum("cte,cde->td", qkv_low, full_qkv, preferred_element_type=jnp.float32)
    )
    grad_in_one, gain_one, shift_one = pull_one(grad_hidden_one)
    grad_tokens = grad_after_self + grad_in_one
    gain_terms = jnp.stack([gain_one, gain_two, gain_three, gain_four])
    shift_terms = jnp.stack([shift_one, shift_two, shift_three, shift_four])
    bias_terms = jnp.stack(
        [
            jnp.sum(grad_after_self, axis=0),
            jnp.sum(grad_after_cross, axis=0),
            jnp.sum(grad_mlp, axis=0),
        ]
    )
    gain_total, shift_total, bias_total, up_total = (
        lax.psum(gain_terms.astype(jnp.bfloat16), "dp").astype(jnp.float32),
        lax.psum(shift_terms.astype(jnp.bfloat16), "dp").astype(jnp.float32),
        lax.psum(bias_terms.astype(jnp.bfloat16), "dp").astype(jnp.float32),
        lax.psum(up_bias_grad.astype(jnp.bfloat16), "dp").astype(jnp.float32),
    )
    sum_qkv, sum_wout, sum_cq, sum_ckv, sum_cout, sum_up, sum_down = (
        lax.psum_scatter(
            grad_qkv.astype(jnp.bfloat16), "dp", scatter_dimension=1, tiled=True
        ).astype(jnp.float32),
        lax.psum_scatter(
            grad_wout.astype(jnp.bfloat16), "dp", scatter_dimension=1, tiled=True
        ).astype(jnp.float32),
        lax.psum_scatter(
            grad_cq.astype(jnp.bfloat16), "dp", scatter_dimension=0, tiled=True
        ).astype(jnp.float32),
        lax.psum_scatter(
            grad_ckv.astype(jnp.bfloat16), "dp", scatter_dimension=1, tiled=True
        ).astype(jnp.float32),
        lax.psum_scatter(
            grad_cout.astype(jnp.bfloat16), "dp", scatter_dimension=1, tiled=True
        ).astype(jnp.float32),
        lax.psum_scatter(
            grad_up.astype(jnp.bfloat16), "dp", scatter_dimension=0, tiled=True
        ).astype(jnp.float32),
        lax.psum_scatter(
            grad_down.astype(jnp.bfloat16), "dp", scatter_dimension=1, tiled=True
        ).astype(jnp.float32),
    )
    return (
        output,
        grad_tokens,
        grad_text,
        sum_qkv,
        sum_wout,
        sum_cq,
        sum_ckv,
        sum_cout,
        sum_up,
        sum_down,
        gain_total,
        shift_total,
        bias_total,
        up_total,
    )


def solution(mesh):
    in_specs = (
        P("dp", None),
        P("dp", "mp"),
        P("dp", None),
        P("dp", None),
        P(None, "dp", "mp"),
        P("mp", "dp"),
        P("dp", "mp"),
        P(None, "dp", "mp"),
        P("mp", "dp"),
        P("dp", "mp"),
        P("mp", "dp"),
        P(),
        P(),
        P(),
        P("mp"),
        P("dp", None),
    )
    out_specs = (
        P("dp", None),
        P("dp", None),
        P("dp", "mp"),
        P(None, "dp", "mp"),
        P("mp", "dp"),
        P("dp", "mp"),
        P(None, "dp", "mp"),
        P("mp", "dp"),
        P("dp", "mp"),
        P("mp", "dp"),
        P(),
        P(),
        P(),
        P("mp"),
    )
    return jax.shard_map(
        on_device, mesh=mesh, in_specs=in_specs, out_specs=out_specs, check_vma=False
    )
```

profile of v0, /device:TPU:0, one launch (start us, length us, event | category | flops | bytes accessed | tf_op | source)
XLA Modules:
  0.0 2109.8 jit_solution(6485817762568258638)
XLA Ops:
  13.9 99.0 %all-gather.9.cloned.1.call-done = bf16[3,2048,512]{1,2,0:T(8,128)(2,1)} async-done(((bf16[3,256,512]{1,2,0:T(8,128)(2,1)}), bf16[3,2048,512]{1,2,0:T(8,128)(2,1)}) %all-gather.9.cloned.1.call-update) | async-done | bytes 6291472 | tf_op jit(solution)/shard_map/all_gather | solution.py:110
  124.3 39.2 %all-gather.11.cloned.1.call-done = bf16[512,2048]{1,0:T(8,128)(2,1)} async-done(((bf16[512,256]{1,0:T(8,128)(2,1)}), bf16[512,2048]{1,0:T(8,128)(2,1)}) %all-gather.11.cloned.1.call-update) | async-done | bytes 2097168 | tf_op jit(solution)/shard_map/all_gather | solution.py:111
  172.5 79.7 %all-reduce.8.cloned.1.call-done = f32[512,2048]{1,0:T(8,128)} async-done(((f32[512,2048]{1,0:T(8,128)}), f32[512,2048]{1,0:T(8,128)}) %all-reduce.8.cloned.1.call-update) | async-done | bytes 4194320 | tf_op jit(solution)/shard_map/psum | solution.py:26
  257.8 45.6 %all-gather.17.cloned.1.call-done = bf16[2048,512]{1,0:T(8,128)(2,1)} async-done(((bf16[256,512]{1,0:T(8,128)(2,1)}), bf16[2048,512]{1,0:T(8,128)(2,1)}) %all-gather.17.cloned.1.call-update) | async-done | bytes 2097168 | tf_op jit(solution)/shard_map/all_gather | solution.py:112
  306.4 19.6 all-gather.15.cloned.1.call-done
  326.0 127.4 %all-gather.13.cloned.1.call-done = bf16[2,4096,512]{1,2,0:T(8,128)(2,1)} async-done(((bf16[2,512,512]{1,2,0:T(8,128)(2,1)}), bf16[2,4096,512]{1,2,0:T(8,128)(2,1)}) %all-gather.13.cloned.1.call-update) | async-done | bytes 8388624 | tf_op jit(solution)/shard_map/all_gather | solution.py:113
  461.3 42.8 %all-gather.19.cloned.1.call-done = bf16[512,2048]{1,0:T(8,128)(2,1)} async-done(((bf16[512,256]{1,0:T(8,128)(2,1)}), bf16[512,2048]{1,0:T(8,128)(2,1)}) %all-gather.19.cloned.1.call-update) | async-done | bytes 2097168 | tf_op jit(solution)/shard_map/all_gather | solution.py:114
  510.5 82.3 %all-reduce.10.cloned.1.call-done = f32[512,2048]{1,0:T(8,128)} async-done(((f32[512,2048]{1,0:T(8,128)}), f32[512,2048]{1,0:T(8,128)}) %all-reduce.10.cloned.1.call-update) | async-done | bytes 4194320 | tf_op jit(solution)/shard_map/psum | solution.py:26
  599.3 120.2 %all-gather.21.cloned.1.call-done = bf16[2048,2048]{1,0:T(8,128)(2,1)} async-done(((bf16[256,2048]{1,0:T(8,128)(2,1)}), bf16[2048,2048]{1,0:T(8,128)(2,1)}) %all-gather.21.cloned.1.call-update) | async-done | bytes 8388624 | tf_op jit(solution)/shard_map/all_gather | solution.py:115
  730.7 113.8 %all-gather.23.cloned.1.call-done = bf16[2048,2048]{1,0:T(8,128)(2,1)} async-done(((bf16[2048,256]{1,0:T(8,128)(2,1)}), bf16[2048,2048]{1,0:T(8,128)(2,1)}) %all-gather.23.cloned.1.call-update) | async-done | bytes 8388624 | tf_op jit(solution)/shard_map/all_gather | solution.py:116
  856.4 83.6 %all-reduce.12.cloned.1.call-done = f32[512,2048]{1,0:T(8,128)} async-done(((f32[512,2048]{1,0:T(8,128)}), f32[512,2048]{1,0:T(8,128)}) %all-reduce.12.cloned.1.call-update) | async-done | bytes 4194320 | tf_op jit(solution)/shard_map/psum | solution.py:26
  969.7 85.5 %all-reduce.14.cloned.1.call-done = f32[512,2048]{1,0:T(8,128)} async-done(((f32[512,2048]{1,0:T(8,128)}), f32[512,2048]{1,0:T(8,128)}) %all-reduce.14.cloned.1.call-update) | async-done | bytes 4194320 | tf_op jit(solution)/shard_map/psum | solution.py:30
  1072.5 85.2 %all-reduce.16.cloned.1.call-done = f32[512,2048]{1,0:T(8,128)} async-done(((f32[512,2048]{1,0:T(8,128)}), f32[512,2048]{1,0:T(8,128)}) %all-reduce.16.cloned.1.call-update) | async-done | bytes 4194320 | tf_op jit(solution)/shard_map/psum | solution.py:30
  1218.7 12.4 convolution_convert_fusion
  1260.7 16.9 all-reduce.18.cloned.1.call-done
  1283.1 38.6 %all-reduce = (bf16[4,2048]{1,0:T(4,128)(2,1)S(1)}, bf16[4,2048]{1,0:T(4,128)(2,1)S(1)}, bf16[3,2048]{1,0:T(4,128)(2,1)S(1)}, bf16[2048]{0:T(1024)(128)(2,1)S(1)}) all-reduce(bf16[4,2048]{1,0:T(4,128)(2,1)S(1)} %get-tuple-element.190, bf16[4,2048]{1,0:T(4,128)(2,1)S(1)} %get-tuple-element.191, ...), channel_id=1, replica_groups=mesh['dp'=8,'mp'=4] {'dp'}, use_global_device_ids=true, to_apply=%region_40.41 | all-reduce | flops 24576 | bytes 98304 | tf_op jit(solution)/shard_map/psum | solution.py:249
  1329.8 20.3 reduce-scatter.15.cloned.1.call-done
  1352.0 31.5 %reduce-scatter.9.cloned.1.call-done = bf16[256,1024]{1,0:T(8,128)(2,1)} async-done(((bf16[256,4096]{1,0:T(8,128)(2,1)}), bf16[256,1024]{1,0:T(8,128)(2,1)}) %reduce-scatter.9.cloned.1.call-update) | async-done | bytes 524304 | tf_op jit(solution)/shard_map/reduce_scatter | solution.py:207
  1385.6 70.2 %reduce-scatter.19.cloned.1.call-done = bf16[512,256]{1,0:T(8,128)(2,1)} async-done(((bf16[512,2048]{1,0:T(8,128)(2,1)}), bf16[512,256]{1,0:T(8,128)(2,1)}) %reduce-scatter.19.cloned.1.call-update) | async-done | bytes 262160 | tf_op jit(solution)/shard_map/reduce_scatter | solution.py:267
  1457.5 70.0 %reduce-scatter.13.cloned.1.call-done = bf16[512,256]{1,0:T(8,128)(2,1)} async-done(((bf16[512,2048]{1,0:T(8,128)(2,1)}), bf16[512,256]{1,0:T(8,128)(2,1)}) %reduce-scatter.13.cloned.1.call-update) | async-done | bytes 262160 | tf_op jit(solution)/shard_map/reduce_scatter | solution.py:258
  1529.3 148.7 %reduce-scatter.23.cloned.1.call-done = bf16[2048,256]{1,0:T(8,128)(2,1)} async-done(((bf16[2048,2048]{1,0:T(8,128)(2,1)}), bf16[2048,256]{1,0:T(8,128)(2,1)}) %reduce-scatter.23.cloned.1.call-update) | async-done | bytes 1048592 | tf_op jit(solution)/shard_map/reduce_scatter | solution.py:273
  1680.8 147.4 %reduce-scatter.21.cloned.1.call-done = bf16[256,2048]{1,0:T(8,128)(2,1)} async-done(((bf16[2048,2048]{1,0:T(8,128)(2,1)}), bf16[256,2048]{1,0:T(8,128)(2,1)}) %reduce-scatter.21.cloned.1.call-update) | async-done | bytes 1048592 | tf_op jit(solution)/shard_map/reduce_scatter | solution.py:270
  1830.9 118.5 %reduce-scatter.11.cloned.1.call-done = bf16[3,256,512]{1,2,0:T(8,128)(2,1)} async-done(((bf16[3,2048,512]{1,2,0:T(8,128)(2,1)}), bf16[3,256,512]{1,2,0:T(8,128)(2,1)}) %reduce-scatter.11.cloned.1.call-update) | async-done | bytes 786448 | tf_op jit(solution)/shard_map/reduce_scatter | solution.py:255
  1951.9 148.2 %reduce-scatter.17.cloned.1.call-done = bf16[2,512,512]{1,2,0:T(8,128)(2,1)} async-done(((bf16[2,4096,512]{1,2,0:T(8,128)(2,1)}), bf16[2,512,512]{1,2,0:T(8,128)(2,1)}) %reduce-scatter.17.cloned.1.call-update) | async-done | bytes 1048592 | tf_op jit(solution)/shard_map/reduce_scatter | solution.py:264
  (273 shorter events, 247.6 us)
Async XLA Ops:
  7.2 105.7 %all-gather.9.cloned.1.call-start = ((), (), s32[]{:S(2)}) async-start(), calls=%async_computation.8 | async-start | bytes 7077888 | tf_op jit(solution)/shard_map/all_gather | solution.py:110
  9.7 153.8 %all-gather.11.cloned.1.call-start = ((), (), s32[]{:S(2)}) async-start(), calls=%async_computation.9 | async-start | bytes 2359296 | tf_op jit(solution)/shard_map/all_gather | solution.py:111
  10.5 241.7 %all-reduce.8.cloned.1.call-start = ((), (), s32[]{:S(2)}) async-start(), calls=%async_computation.10 | async-start | bytes 8388608 | tf_op jit(solution)/shard_map/psum | solution.py:26
  168.4 135.1 %all-gather.17.cloned.1.call-start = ((), (), s32[]{:S(2)}) async-start(), calls=%async_computation.13 | async-start | bytes 2359296 | tf_op jit(solution)/shard_map/all_gather | solution.py:112
  169.0 157.0 %all-gather.15.cloned.1.call-start = ((), (), s32[]{:S(2)}) async-start(), calls=%async_computation.12 | async-start | bytes 2621440 | tf_op jit(solution)/shard_map/all_gather | solution.py:119
  169.6 283.9 %all-gather.13.cloned.1.call-start = ((), (), s32[]{:S(2)}) async-start(), calls=%async_computation.11 | async-start | bytes 9437184 | tf_op jit(solution)/shard_map/all_gather | solution.py:113
  171.0 333.1 %all-gather.19.cloned.1.call-start = ((), (), s32[]{:S(2)}) async-start(), calls=%async_computation.14 | async-start | bytes 2359296 | tf_op jit(solution)/shard_map/all_gather | solution.py:114
  171.7 421.0 %all-reduce.10.cloned.1.call-start = ((), (), s32[]{:S(2)}) async-start(), calls=%async_computation.15 | async-start | bytes 8388608 | tf_op jit(solution)/shard_map/psum | solution.py:26
  306.4 153.5 %copy-start.26 = (bf16[512,512]{0,1:T(8,128)(2,1)}, bf16[512,512]{0,1:T(8,128)(2,1)S(1)}, u32[]{:S(2)}) copy-start(bf16[512,512]{0,1:T(8,128)(2,1)S(1)} %convolution_convert_fusion.9) | copy-start | bytes 1572868
  508.9 210.6 %all-gather.21.cloned.1.call-start = ((), (), s32[]{:S(2)}) async-start(), calls=%async_computation.16 | async-start | bytes 9437184 | tf_op jit(solution)/shard_map/all_gather | solution.py:115
  509.7 334.9 %all-gather.23.cloned.1.call-start = ((), (), s32[]{:S(2)}) async-start(), calls=%async_computation.17 | async-start | bytes 9437184 | tf_op jit(solution)/shard_map/all_gather | solution.py:116
  510.2 429.7 %all-reduce.12.cloned.1.call-start = ((), (), s32[]{:S(2)}) async-start(), calls=%async_computation.18 | async-start | bytes 8388608 | tf_op jit(solution)/shard_map/psum | solution.py:26
  719.5 125.0 %copy-start.51 = (f32[2048]{0:T(1024)S(1)}, f32[2048]{0:T(1024)}, u32[]{:S(2)}) copy-start(f32[2048]{0:T(1024)} %param.30) | copy-start | bytes 24580
  856.1 199.1 %all-reduce.14.cloned.1.call-start = ((), (), s32[]{:S(2)}) async-start(), calls=%async_computation.19 | async-start | bytes 8388608 | tf_op jit(solution)/shard_map/psum | solution.py:30
  969.4 188.3 %all-reduce.16.cloned.1.call-start = ((), (), s32[]{:S(2)}) async-start(), calls=%async_computation.20 | async-start | bytes 8388608 | tf_op jit(solution)/shard_map/psum | solution.py:30
  1071.9 205.7 %all-reduce.18.cloned.1.call-start = ((), (), s32[]{:S(2)}) async-start(), calls=%async_computation.21 | async-start | bytes 8388608 | tf_op jit(solution)/shard_map/psum | solution.py:30
  1191.8 158.3 %reduce-scatter.15.cloned.1.call-start = ((), (), s32[]{:S(2)}) async-start(), calls=%async_computation.25 | async-start | bytes 2359296 | tf_op jit(solution)/shard_map/reduce_scatter | solution.py:261
  1196.2 187.2 %reduce-scatter.9.cloned.1.call-start = ((), (), s32[]{:S(2)}) async-start(), calls=%async_computation.22 | async-start | bytes 2621440 | tf_op jit(solution)/shard_map/reduce_scatter | solution.py:207
  1208.7 247.0 %reduce-scatter.19.cloned.1.call-start = ((), (), s32[]{:S(2)}) async-start(), calls=%async_computation.27 | async-start | bytes 2359296 | tf_op jit(solution)/shard_map/reduce_scatter | solution.py:267
  1213.7 313.9 %reduce-scatter.13.cloned.1.call-start = ((), (), s32[]{:S(2)}) async-start(), calls=%async_computation.24 | async-start | bytes 2359296 | tf_op jit(solution)/shard_map/reduce_scatter | solution.py:258
  1218.6 459.5 %reduce-scatter.23.cloned.1.call-start = ((), (), s32[]{:S(2)}) async-start(), calls=%async_computation.29 | async-start | bytes 9437184 | tf_op jit(solution)/shard_map/reduce_scatter | solution.py:273
  1231.1 597.1 %reduce-scatter.21.cloned.1.call-start = ((), (), s32[]{:S(2)}) async-start(), calls=%async_computation.28 | async-start | bytes 9437184 | tf_op jit(solution)/shard_map/reduce_scatter | solution.py:270
  1242.2 707.2 %reduce-scatter.11.cloned.1.call-start = ((), (), s32[]{:S(2)}) async-start(), calls=%async_computation.23 | async-start | bytes 7077888 | tf_op jit(solution)/shard_map/reduce_scatter | solution.py:255
  1251.2 849.0 %reduce-scatter.17.cloned.1.call-start = ((), (), s32[]{:S(2)}) async-start(), calls=%async_computation.26 | async-start | bytes 9437184 | tf_op jit(solution)/shard_map/reduce_scatter | solution.py:264
  (55 other events, 751.6 us)
Sparse Core Ops, SparseCore 0:
  10.6 102.1 all-gather.8
  114.9 48.5 all-gather.10
  168.5 83.6 all-reduce.7
  254.2 49.2 all-gather.16
  304.9 21.0 all-gather.14
  328.5 124.9 all-gather.12
  455.5 48.5 all-gather.18
  509.0 83.6 all-reduce.9
  594.9 124.6 all-gather.20
  721.4 123.1 all-gather.22
  856.2 83.6 all-reduce.11
  969.5 85.6 all-reduce.13
  1072.1 85.6 all-reduce.15
  1191.9 85.6 all-reduce.17
  1281.5 68.5 reduce-scatter.14
  1353.1 30.2 reduce-scatter.8
  1386.8 68.8 reduce-scatter.18
  1459.7 67.8 reduce-scatter.12
  1531.2 146.8 reduce-scatter.22
  1681.6 146.5 reduce-scatter.20
  1831.8 117.5 reduce-scatter.10
  1953.0 147.0 reduce-scatter.16
where the time goes:
time: 2120 us; the launch traced here: 2110 us
  waiting for transfers between devices  1800 us (85%)
  matrix products  151 us (7%)
  other arithmetic  65.1 us (3%)
  blocking collectives  38.6 us (2%)
  local copies, waits for them, and re-layouts  36.8 us (2%)
    psum x3, waiting for transfers between devices, heads_sum(): return lax.psum(partial_value, 'mp')  246 us
    psum x3, waiting for transfers between devices, input_sum(): return lax.psum(partial_value, 'mp')  188 us
    reduce_scatter x1, waiting for transfers between devices, on_device(): lax.psum_scatter(grad_down.astype(jnp.bfloat16), 'dp', scatter_dimension=...  149 us
    reduce_scatter x1, waiting for transfers between devices, on_device(): lax.psum_scatter(grad_ckv.astype(jnp.bfloat16), 'dp', scatter_dimension=1...  148 us
    reduce_scatter x1, waiting for transfers between devices, on_device(): lax.psum_scatter(grad_up.astype(jnp.bfloat16), 'dp', scatter_dimension=0,...  147 us
    all_gather x1, waiting for transfers between devices, on_device(): lax.all_gather(c_kv, 'dp', axis=1, tiled=True)  127 us
    all_gather x1, waiting for transfers between devices, on_device(): lax.all_gather(w_up, 'dp', axis=0, tiled=True)  120 us
    reduce_scatter x1, waiting for transfers between devices, on_device(): lax.psum_scatter(grad_qkv.astype(jnp.bfloat16), 'dp', scatter_dimension=1...  118 us
  transfers between devices with their start and end apart: 22, of which 22 were waited for; matrix products, arithmetic and copies ran while one was open for 7% of the time, Pallas kernels for 0%

commit v1 on v0

--- a/solution.py
+++ b/solution.py
@@ -6,6 +6,28 @@
 HD = 128
 eps = 1e-05
 masked = -1e30
+
+
+def laid_out(blocks, dim):
+    blocks = jnp.moveaxis(blocks, 0, dim)
+    shape = blocks.shape
+    return blocks.reshape(*shape[:dim], shape[dim] * shape[dim + 1], *shape[dim + 2 :])
+
+
+def ring_gather(array, axis, dim):
+    length = lax.axis_size(axis)
+    pairs = [(i, (i + 1) % length) for i in range(length)]
+    back = [(b, a) for a, b in pairs]
+    lower, upper = ([], [])
+    for turn in range(length - 1):
+        if turn % 2 == 0:
+            lower.append(lax.ppermute(lower[-1] if lower else array, axis, pairs))
+        else:
+            upper.append(lax.ppermute(upper[-1] if upper else array, axis, back))
+    blocks = jnp.stack([*lower[::-1], array, *upper])
+    shift = lax.axis_index(axis) - len(lower)
+    blocks = blocks[(jnp.arange(length) - shift) % length]
+    return laid_out(blocks, dim)
 
 
 def normalize(values, gain, shift):
@@ -113,7 +135,7 @@
         lax.all_gather(c_kv, "dp", axis=1, tiled=True),
         lax.all_gather(c_out, "dp", axis=1, tiled=True),
         lax.all_gather(w_up, "dp", axis=0, tiled=True),
-        lax.all_gather(w_down, "dp", axis=1, tiled=True),
+        ring_gather(w_down, "dp", 1),
     )
     full_qkv, full_out, full_cq, full_ckv, full_cout, full_up, full_down = gathered
     words = lax.all_gather(text, "mp", axis=1, tiled=True)

time: 2120 us -> 2040 us (0.962)
  waiting for transfers between devices: 1800 us -> 1650 us
  starting transfers between devices: 2.9 us -> 49.7 us
  local copies, waits for them, and re-layouts: 36.8 us -> 68.3 us
    ppermute x0 -> x7, waiting for transfers between devices: none -> 131 us  [the longest x4 119 us: ring_gather(): lower.append(lax.ppermute(lower[-1] if lower else array, axis, pairs))]
    all_gather x1 -> x0, waiting for transfers between devices: 114 us -> none  [on_device(): lax.all_gather(w_down, 'dp', axis=1, tiled=True)]
    all_gather x1, waiting for transfers between devices: 120 us -> 32.1 us  [on_device(): lax.all_gather(w_up, 'dp', axis=0, tiled=True)]
    psum x3, waiting for transfers between devices: 246 us -> 164 us  [heads_sum(): return lax.psum(partial_value, 'mp')]
    ppermute x0 -> x7, starting transfers between devices: none -> 47.1 us  [the longest x3 40.5 us: ring_gather(): upper.append(lax.ppermute(upper[-1] if upper else array, axis, back))]
    reduce_scatter x1, waiting for transfers between devices: 20.3 us -> 52.6 us  [on_device(): lax.psum_scatter(grad_cq.astype(jnp.bfloat16), 'dp', scatter_dimension=0,...]
    reduce_scatter x1, waiting for transfers between devices: 31.5 us -> 0.01 us  [on_device(): lax.psum_scatter(text_term.astype(jnp.bfloat16), 'mp', scatter_dimension=...]
  transfers between devices with their start and end apart: 22 -> 28, of which waited for: 22 -> 24; matrix products, arithmetic and copies ran while one was open for 7% -> 8% of each run, Pallas kernels for 0% -> 0%
where the time goes in v1:
time: 2040 us
  waiting for transfers between devices  1650 us (81%)
  matrix products  149 us (7%)
  local copies, waits for them, and re-layouts  68.3 us (3%)
  other arithmetic  64.9 us (3%)
  starting transfers between devices  49.7 us (2%)
  blocking collectives  37.6 us (2%)
    psum x3, waiting for transfers between devices, input_sum(): return lax.psum(partial_value, 'mp')  190 us
    psum x3, waiting for transfers between devices, heads_sum(): return lax.psum(partial_value, 'mp')  164 us
    reduce_scatter x1, waiting for transfers between devices, on_device(): lax.psum_scatter(grad_ckv.astype(jnp.bfloat16), 'dp', scatter_dimension=1...  148 us
    reduce_scatter x1, waiting for transfers between devices, on_device(): lax.psum_scatter(grad_up.astype(jnp.bfloat16), 'dp', scatter_dimension=0,...  148 us
    reduce_scatter x1, waiting for transfers between devices, on_device(): lax.psum_scatter(grad_down.astype(jnp.bfloat16), 'dp', scatter_dimension=...  148 us
    all_gather x1, waiting for transfers between devices, on_device(): lax.all_gather(c_kv, 'dp', axis=1, tiled=True)  127 us
    ppermute x4, waiting for transfers between devices, ring_gather(): lower.append(lax.ppermute(lower[-1] if lower else array, axis, pairs))  119 us
    reduce_scatter x1, waiting for transfers between devices, on_device(): lax.psum_scatter(grad_qkv.astype(jnp.bfloat16), 'dp', scatter_dimension=1...  119 us
  transfers between devices with their start and end apart: 28, of which 24 were waited for; matrix products, arithmetic and copies ran while one was open for 8% of the time, Pallas kernels for 0%

profile of v1, /device:TPU:0, one launch (start us, length us, event | category | flops | bytes accessed | tf_op | source)
XLA Modules:
  0.0 2035.1 jit_solution(12705034824884164918)
XLA Ops:
  13.9 99.0 %all-gather.8.cloned.1.call-done = bf16[3,2048,512]{1,2,0:T(8,128)(2,1)} async-done(((bf16[3,256,512]{1,2,0:T(8,128)(2,1)}), bf16[3,2048,512]{1,2,0:T(8,128)(2,1)}) %all-gather.8.cloned.1.call-update) | async-done | bytes 6291472 | tf_op jit(solution)/shard_map/all_gather | solution.py:132
  124.3 39.1 %all-gather.10.cloned.1.call-done = bf16[512,2048]{1,0:T(8,128)(2,1)} async-done(((bf16[512,256]{1,0:T(8,128)(2,1)}), bf16[512,2048]{1,0:T(8,128)(2,1)}) %all-gather.10.cloned.1.call-update) | async-done | bytes 2097168 | tf_op jit(solution)/shard_map/all_gather | solution.py:133
  172.2 80.0 %all-reduce.8.cloned.1.call-done = f32[512,2048]{1,0:T(8,128)} async-done(((f32[512,2048]{1,0:T(8,128)}), f32[512,2048]{1,0:T(8,128)}) %all-reduce.8.cloned.1.call-update) | async-done | bytes 4194320 | tf_op jit(solution)/shard_map/psum | solution.py:48
  257.9 45.6 %all-gather.16.cloned.1.call-done = bf16[2048,512]{1,0:T(8,128)(2,1)} async-done(((bf16[256,512]{1,0:T(8,128)(2,1)}), bf16[2048,512]{1,0:T(8,128)(2,1)}) %all-gather.16.cloned.1.call-update) | async-done | bytes 2097168 | tf_op jit(solution)/shard_map/all_gather | solution.py:134
  306.4 19.6 all-gather.14.cloned.1.call-done
  326.0 127.4 %all-gather.12.cloned.1.call-done = bf16[2,4096,512]{1,2,0:T(8,128)(2,1)} async-done(((bf16[2,512,512]{1,2,0:T(8,128)(2,1)}), bf16[2,4096,512]{1,2,0:T(8,128)(2,1)}) %all-gather.12.cloned.1.call-update) | async-done | bytes 8388624 | tf_op jit(solution)/shard_map/all_gather | solution.py:135
  461.3 42.7 %all-gather.18.cloned.1.call-done = bf16[512,2048]{1,0:T(8,128)(2,1)} async-done(((bf16[512,256]{1,0:T(8,128)(2,1)}), bf16[512,2048]{1,0:T(8,128)(2,1)}) %all-gather.18.cloned.1.call-update) | async-done | bytes 2097168 | tf_op jit(solution)/shard_map/all_gather | solution.py:136
  511.5 25.3 %collective-permute-done = bf16[2048,256]{1,0:T(8,128)(2,1)S(1)} collective-permute-done((bf16[2048,256]{1,0:T(8,128)(2,1)S(1)}, bf16[2048,256]{1,0:T(8,128)(2,1)S(1)}, u32[]{:S(2)}, u32[]{:S(2)}) %collective-permute-start) | collective-permute-done | bytes 1048608 | tf_op jit(solution)/shard_map/ppermute | solution.py:24
  541.5 39.2 %collective-permute-done.1 = bf16[2048,256]{1,0:T(8,128)(2,1)S(1)} collective-permute-done((bf16[2048,256]{1,0:T(8,128)(2,1)S(1)}, bf16[2048,256]{1,0:T(8,128)(2,1)S(1)}, u32[]{:S(2)}, u32[]{:S(2)}) %collective-permute-start.1) | collective-permute-done | bytes 1048608 | tf_op jit(solution)/shard_map/ppermute | solution.py:24
  583.2 23.0 %collective-permute-start.5 = (bf16[2048,256]{1,0:T(8,128)(2,1)}, bf16[2048,256]{1,0:T(8,128)(2,1)}, u32[]{:S(2)}, u32[]{:S(2)}) collective-permute-start(bf16[2048,256]{1,0:T(8,128)(2,1)} %collective-permute-done.4), channel_id=1, source_target_pairs={{4,0},{8,4},{12,8},{16,12},{20,16},{24,20},{28,24},{0,28},{5,1},{9... | collective-permute-start | bytes 3145736 | tf_op jit(solution)/shard_map/ppermute | solution.py:26
  606.3 31.4 %collective-permute-done.2 = bf16[2048,256]{1,0:T(8,128)(2,1)} collective-permute-done((bf16[2048,256]{1,0:T(8,128)(2,1)S(1)}, bf16[2048,256]{1,0:T(8,128)(2,1)}, u32[]{:S(2)}, u32[]{:S(2)}) %collective-permute-start.2) | collective-permute-done | bytes 1048608 | tf_op jit(solution)/shard_map/ppermute | solution.py:24
  665.1 23.5 %collective-permute-done.3 = bf16[2048,256]{1,0:T(8,128)(2,1)} collective-permute-done((bf16[2048,256]{1,0:T(8,128)(2,1)}, bf16[2048,256]{1,0:T(8,128)(2,1)}, u32[]{:S(2)}, u32[]{:S(2)}) %collective-permute-start.3) | collective-permute-done | bytes 1048608 | tf_op jit(solution)/shard_map/ppermute | solution.py:24
  728.2 32.1 %all-gather.20.cloned.1.call-done = bf16[2048,2048]{1,0:T(8,128)(2,1)} async-done(((bf16[256,2048]{1,0:T(8,128)(2,1)}), bf16[2048,2048]{1,0:T(8,128)(2,1)}) %all-gather.20.cloned.1.call-update) | async-done | bytes 8388624 | tf_op jit(solution)/shard_map/all_gather | solution.py:137
  780.9 84.4 %all-reduce.12.cloned.1.call-done = f32[512,2048]{1,0:T(8,128)} async-done(((f32[512,2048]{1,0:T(8,128)}), f32[512,2048]{1,0:T(8,128)}) %all-reduce.12.cloned.1.call-update) | async-done | bytes 4194320 | tf_op jit(solution)/shard_map/psum | solution.py:48
  895.9 85.5 %all-reduce.14.cloned.1.call-done = f32[512,2048]{1,0:T(8,128)} async-done(((f32[512,2048]{1,0:T(8,128)}), f32[512,2048]{1,0:T(8,128)}) %all-reduce.14.cloned.1.call-update) | async-done | bytes 4194320 | tf_op jit(solution)/shard_map/psum | solution.py:52
  998.5 85.5 %all-reduce.16.cloned.1.call-done = f32[512,2048]{1,0:T(8,128)} async-done(((f32[512,2048]{1,0:T(8,128)}), f32[512,2048]{1,0:T(8,128)}) %all-reduce.16.cloned.1.call-update) | async-done | bytes 4194320 | tf_op jit(solution)/shard_map/psum | solution.py:52
  1209.4 37.6 %all-reduce = (bf16[4,2048]{1,0:T(4,128)(2,1)S(1)}, bf16[4,2048]{1,0:T(4,128)(2,1)S(1)}, bf16[3,2048]{1,0:T(4,128)(2,1)S(1)}, bf16[2048]{0:T(1024)(128)(2,1)S(1)}) all-reduce(bf16[4,2048]{1,0:T(4,128)(2,1)S(1)} %get-tuple-element.218, bf16[4,2048]{1,0:T(4,128)(2,1)S(1)} %get-tuple-element.219, ...), channel_id=1, replica_groups=mesh['dp'=8,'mp'=4] {'dp'}, use_global_device_ids=true, to_apply=%region_40.41 | all-reduce | flops 24576 | bytes 98304 | tf_op jit(solution)/shard_map/psum | solution.py:271
  1257.2 52.6 %reduce-scatter.15.cloned.1.call-done = bf16[256,512]{1,0:T(8,128)(2,1)} async-done(((bf16[2048,512]{1,0:T(8,128)(2,1)}), bf16[256,512]{1,0:T(8,128)(2,1)}) %reduce-scatter.15.cloned.1.call-update) | async-done | bytes 262160 | tf_op jit(solution)/shard_map/reduce_scatter | solution.py:283
  1311.7 69.5 %reduce-scatter.19.cloned.1.call-done = bf16[512,256]{1,0:T(8,128)(2,1)} async-done(((bf16[512,2048]{1,0:T(8,128)(2,1)}), bf16[512,256]{1,0:T(8,128)(2,1)}) %reduce-scatter.19.cloned.1.call-update) | async-done | bytes 262160 | tf_op jit(solution)/shard_map/reduce_scatter | solution.py:289
  1382.9 70.1 %reduce-scatter.13.cloned.1.call-done = bf16[512,256]{1,0:T(8,128)(2,1)} async-done(((bf16[512,2048]{1,0:T(8,128)(2,1)}), bf16[512,256]{1,0:T(8,128)(2,1)}) %reduce-scatter.13.cloned.1.call-update) | async-done | bytes 262160 | tf_op jit(solution)/shard_map/reduce_scatter | solution.py:280
  1454.8 119.2 %reduce-scatter.11.cloned.1.call-done = bf16[3,256,512]{1,2,0:T(8,128)(2,1)} async-done(((bf16[3,2048,512]{1,2,0:T(8,128)(2,1)}), bf16[3,256,512]{1,2,0:T(8,128)(2,1)}) %reduce-scatter.11.cloned.1.call-update) | async-done | bytes 786448 | tf_op jit(solution)/shard_map/reduce_scatter | solution.py:277
  1576.5 147.8 %reduce-scatter.21.cloned.1.call-done = bf16[256,2048]{1,0:T(8,128)(2,1)} async-done(((bf16[2048,2048]{1,0:T(8,128)(2,1)}), bf16[256,2048]{1,0:T(8,128)(2,1)}) %reduce-scatter.21.cloned.1.call-update) | async-done | bytes 1048592 | tf_op jit(solution)/shard_map/reduce_scatter | solution.py:292
  1727.1 147.7 %reduce-scatter.23.cloned.1.call-done = bf16[2048,256]{1,0:T(8,128)(2,1)} async-done(((bf16[2048,2048]{1,0:T(8,128)(2,1)}), bf16[2048,256]{1,0:T(8,128)(2,1)}) %reduce-scatter.23.cloned.1.call-update) | async-done | bytes 1048592 | tf_op jit(solution)/shard_map/reduce_scatter | solution.py:295
  1877.5 147.9 %reduce-scatter.17.cloned.1.call-done = bf16[2,512,512]{1,2,0:T(8,128)(2,1)} async-done(((bf16[2,4096,512]{1,2,0:T(8,128)(2,1)}), bf16[2,512,512]{1,2,0:T(8,128)(2,1)}) %reduce-scatter.17.cloned.1.call-update) | async-done | bytes 1048592 | tf_op jit(solution)/shard_map/reduce_scatter | solution.py:286
  (311 shorter events, 343.8 us)
Async XLA Ops:
  7.2 105.7 %all-gather.8.cloned.1.call-start = ((), (), s32[]{:S(2)}) async-start(), calls=%async_computation.8 | async-start | bytes 7077888 | tf_op jit(solution)/shard_map/all_gather | solution.py:132
  9.7 153.8 %all-gather.10.cloned.1.call-start = ((), (), s32[]{:S(2)}) async-start(), calls=%async_computation.9 | async-start | bytes 2359296 | tf_op jit(solution)/shard_map/all_gather | solution.py:133
  10.5 241.7 %all-reduce.8.cloned.1.call-start = ((), (), s32[]{:S(2)}) async-start(), calls=%async_computation.10 | async-start | bytes 8388608 | tf_op jit(solution)/shard_map/psum | solution.py:48
  168.4 135.1 %all-gather.16.cloned.1.call-start = ((), (), s32[]{:S(2)}) async-start(), calls=%async_computation.13 | async-start | bytes 2359296 | tf_op jit(solution)/shard_map/all_gather | solution.py:134
  169.0 157.0 %all-gather.14.cloned.1.call-start = ((), (), s32[]{:S(2)}) async-start(), calls=%async_computation.12 | async-start | bytes 2621440 | tf_op jit(solution)/shard_map/all_gather | solution.py:141
  169.6 283.9 %all-gather.12.cloned.1.call-start = ((), (), s32[]{:S(2)}) async-start(), calls=%async_computation.11 | async-start | bytes 9437184 | tf_op jit(solution)/shard_map/all_gather | solution.py:135
  171.0 333.1 %all-gather.18.cloned.1.call-start = ((), (), s32[]{:S(2)}) async-start(), calls=%async_computation.14 | async-start | bytes 2359296 | tf_op jit(solution)/shard_map/all_gather | solution.py:136
  171.7 550.0 %all-reduce.10.cloned.1.call-start = ((), (), s32[]{:S(2)}) async-start(), calls=%async_computation.15 | async-start | bytes 8388608 | tf_op jit(solution)/shard_map/psum | solution.py:48
  508.9 251.5 %all-gather.20.cloned.1.call-start = ((), (), s32[]{:S(2)}) async-start(), calls=%async_computation.16 | async-start | bytes 9437184 | tf_op jit(solution)/shard_map/all_gather | solution.py:137
  509.6 355.7 %all-reduce.12.cloned.1.call-start = ((), (), s32[]{:S(2)}) async-start(), calls=%async_computation.17 | async-start | bytes 8388608 | tf_op jit(solution)/shard_map/psum | solution.py:48
  580.8 56.9 %collective-permute-start.2 = (bf16[2048,256]{1,0:T(8,128)(2,1)S(1)}, bf16[2048,256]{1,0:T(8,128)(2,1)}, u32[]{:S(2)}, u32[]{:S(2)}) collective-permute-start(bf16[2048,256]{1,0:T(8,128)(2,1)S(1)} %collective-permute-done.1), channel_id=1, source_target_pairs={{0,4},{4,8},{8,12},{12,16},{16,20},{20,24},{24,28},{28,0},{1,5},{5... | collective-permute-start | bytes 3145736 | tf_op jit(solution)/shard_map/ppermute | solution.py:24
  583.2 69.1 %collective-permute-start.5 = (bf16[2048,256]{1,0:T(8,128)(2,1)}, bf16[2048,256]{1,0:T(8,128)(2,1)}, u32[]{:S(2)}, u32[]{:S(2)}) collective-permute-start(bf16[2048,256]{1,0:T(8,128)(2,1)} %collective-permute-done.4), channel_id=1, source_target_pairs={{4,0},{8,4},{12,8},{16,12},{20,16},{24,20},{28,24},{0,28},{5,1},{9... | collective-permute-start | bytes 3145736 | tf_op jit(solution)/shard_map/ppermute | solution.py:26
  637.7 50.9 %collective-permute-start.3 = (bf16[2048,256]{1,0:T(8,128)(2,1)}, bf16[2048,256]{1,0:T(8,128)(2,1)}, u32[]{:S(2)}, u32[]{:S(2)}) collective-permute-start(bf16[2048,256]{1,0:T(8,128)(2,1)} %collective-permute-done.2), channel_id=1, source_target_pairs={{0,4},{4,8},{8,12},{12,16},{16,20},{20,24},{24,28},{28,0},{1,5},{5... | collective-permute-start | bytes 3145736 | tf_op jit(solution)/shard_map/ppermute | solution.py:24
  780.7 200.7 %all-reduce.14.cloned.1.call-start = ((), (), s32[]{:S(2)}) async-start(), calls=%async_computation.18 | async-start | bytes 8388608 | tf_op jit(solution)/shard_map/psum | solution.py:52
  895.6 188.3 %all-reduce.16.cloned.1.call-start = ((), (), s32[]{:S(2)}) async-start(), calls=%async_computation.19 | async-start | bytes 8388608 | tf_op jit(solution)/shard_map/psum | solution.py:52
  998.2 205.7 %all-reduce.18.cloned.1.call-start = ((), (), s32[]{:S(2)}) async-start(), calls=%async_computation.20 | async-start | bytes 8388608 | tf_op jit(solution)/shard_map/psum | solution.py:52
  1118.1 137.0 %reduce-scatter.9.cloned.1.call-start = ((), (), s32[]{:S(2)}) async-start(), calls=%async_computation.21 | async-start | bytes 2621440 | tf_op jit(solution)/shard_map/reduce_scatter | solution.py:229
  1131.1 178.8 %reduce-scatter.15.cloned.1.call-start = ((), (), s32[]{:S(2)}) async-start(), calls=%async_computation.24 | async-start | bytes 2359296 | tf_op jit(solution)/shard_map/reduce_scatter | solution.py:283
  1133.9 247.3 %reduce-scatter.19.cloned.1.call-start = ((), (), s32[]{:S(2)}) async-start(), calls=%async_computation.26 | async-start | bytes 2359296 | tf_op jit(solution)/shard_map/reduce_scatter | solution.py:289
  1139.0 314.0 %reduce-scatter.13.cloned.1.call-start = ((), (), s32[]{:S(2)}) async-start(), calls=%async_computation.23 | async-start | bytes 2359296 | tf_op jit(solution)/shard_map/reduce_scatter | solution.py:280
  1144.1 429.8 %reduce-scatter.11.cloned.1.call-start = ((), (), s32[]{:S(2)}) async-start(), calls=%async_computation.22 | async-start | bytes 7077888 | tf_op jit(solution)/shard_map/reduce_scatter | solution.py:277
  1151.4 572.9 %reduce-scatter.21.cloned.1.call-start = ((), (), s32[]{:S(2)}) async-start(), calls=%async_computation.27 | async-start | bytes 9437184 | tf_op jit(solution)/shard_map/reduce_scatter | solution.py:292
  1162.6 712.2 %reduce-scatter.23.cloned.1.call-start = ((), (), s32[]{:S(2)}) async-start(), calls=%async_computation.28 | async-start | bytes 9437184 | tf_op jit(solution)/shard_map/reduce_scatter | solution.py:295
  1175.0 850.4 %reduce-scatter.17.cloned.1.call-start = ((), (), s32[]{:S(2)}) async-start(), calls=%async_computation.25 | async-start | bytes 9437184 | tf_op jit(solution)/shard_map/reduce_scatter | solution.py:286
  (68 other events, 1286.4 us)
Sparse Core Ops, SparseCore 0:
  10.6 102.1 all-gather.7
  114.9 48.5 all-gather.9
  168.5 83.6 all-reduce.7
  254.2 49.2 all-gather.15
  304.9 21.0 all-gather.13
  328.5 124.9 all-gather.11
  455.5 48.5 all-gather.17
  509.0 83.6 all-reduce.9
  594.8 165.4 all-gather.19
  780.8 84.4 all-reduce.11
  895.7 85.6 all-reduce.13
  998.3 85.6 all-reduce.15
  1118.2 85.6 all-reduce.17
  1206.9 31.2 reduce-scatter.8
  1241.6 68.2 reduce-scatter.14
  1313.3 67.8 reduce-scatter.18
  1385.1 67.8 reduce-scatter.12
  1456.5 117.4 reduce-scatter.10
  1577.6 146.7 reduce-scatter.20
  1727.8 146.9 reduce-scatter.22
  1878.4 146.9 reduce-scatter.16
